TPU v7x, 32 devices: a whole 2x2x4 slice. The times are simulated.
32 devices in a mesh: group: 4 (over z), shard: 8 (over y, x, core).
Axes of the slice: x: 2, y: 2, z: 4, core: 2. Of those that a mesh axis runs over, the one named last changes fastest.
Arguments:
- query_hidden: bfloat16 [32, 32, 768], P(('group', 'shard')), may hold values from -6 to 6
- positive_hidden: bfloat16 [32, 64, 768], P(('group', 'shard')), may hold values from -6 to 6
- passage_store: bfloat16 [256, 64, 768], P('shard'), may hold values from -6 to 6
- negative_ids: int32 [32, 8], P(('group', 'shard')), may hold values from 0 to 255, as said below
- teacher_margins: int32 [32, 8], P(('group', 'shard')), may hold values from -4096 to 4095
- transform_weight: bfloat16 [768, 768], replicated, may hold values from -0.21875 to 0.21875
- vocab_weight: bfloat16 [768, 15360], P(None, 'shard'), may hold values from -0.21875 to 0.21875
- dense_weight: bfloat16 [768, 768], replicated, may hold values from -0.21875 to 0.21875
Outputs:
- student_margin: float32 [32, 8], P(('group', 'shard'))
- dense_grad: float32 [768, 768], replicated
Inputs may be any that keep to these rules, and one draw needn't show every extreme that they name: `negative_ids`: passage p is held by shard index p // 32. Among the 8 negatives of one index of group and shard, every store index is named by none or exactly 2 of them; one store index, drawn from the seed, is named 2 times by every index of group and shard.
All inputs are finite; a program needn't handle non-finite values.
Results may differ from a plain program's by a relative error of at most 0.0029.
Values may be sent and summed in bfloat16 or wider, within the bound.
A program may use at most 128 MiB of HBM per device.

v0:
```python
from functools import partial
import math

import jax
import jax.numpy as jnp
from jax import lax
from jax.sharding import PartitionSpec as P

CAP = 2


def encode(hidden, transform_weight):
    mixed_rows = jnp.dot(hidden, transform_weight, preferred_element_type=jnp.float32)
    active = jax.nn.gelu(mixed_rows, approximate=False)
    centre = jnp.mean(active, axis=-1, keepdims=True)
    spread = jnp.mean(jnp.square(active - centre), axis=-1, keepdims=True)
    return ((active - centre) * lax.rsqrt(spread + 1e-05)).astype(jnp.bfloat16)


def pool_single(sequence, vocab_weight):
    logits = jnp.dot(sequence, vocab_weight, preferred_element_type=jnp.float32)
    return jnp.max(jnp.log1p(jnp.maximum(logits, 0.0)), axis=0)


def pool_sequences(block_rows, offset, vocab_weight):
    return lax.map(partial(pool_single, vocab_weight=vocab_weight), block_rows, batch_size=8)


def add_outer(running, pieces):
    return running + jnp.einsum("rd,re->de", pieces[0], pieces[1], precision=lax.Precision.HIGHEST)


def body(
    query_hidden,
    positive_hidden,
    passage_store,
    negative_ids,
    teacher_margins,
    transform_weight,
    vocab_weight,
    dense_weight,
):
    shards = lax.axis_size("shard")
    queries_dev, negatives = negative_ids.shape
    store_rows, length, width = passage_store.shape
    vocab_total = vocab_weight.shape[1] * shards
    pooler = partial(pool_sequences, vocab_weight=vocab_weight)
    query_coded = encode(query_hidden, transform_weight)
    positive_coded = encode(positive_hidden, transform_weight)
    query_pool = pooler(lax.all_gather(query_coded, "shard", axis=0, tiled=True), jnp.int32(0))
    neg_total = queries_dev * negatives
    flat_ids = negative_ids.reshape(neg_total)
    owner_of = flat_ids // store_rows
    local_row = flat_ids % store_rows
    shard_ids = jnp.arange(shards, dtype=jnp.int32)
    owner_hit = (owner_of[:, None] == shard_ids[None, :]).astype(jnp.int32)
    earlier = jnp.cumsum(owner_hit, axis=0) - owner_hit
    slot_rank = jnp.sum(earlier * owner_hit, axis=1)
    slot_ids = jnp.arange(CAP, dtype=jnp.int32)
    slot_hit = (owner_hit[:, :, None] > 0) & (slot_rank[:, None, None] == slot_ids[None, None, :])
    asked_rows = jnp.sum(jnp.where(slot_hit, local_row[:, None, None], 0), axis=0)
    requests = jnp.where(jnp.any(slot_hit, axis=0), asked_rows, -1)
    asked_for = lax.all_to_all(requests, "shard", split_axis=0, concat_axis=0, tiled=True)
    is_valid = asked_for >= 0
    served = passage_store[jnp.clip(asked_for, 0, store_rows - 1)]
    served = jnp.where(is_valid[:, :, None, None], served, jnp.zeros((), served.dtype))
    fetched = lax.all_to_all(served, "shard", split_axis=0, concat_axis=0, tiled=True)
    negative_hidden = fetched.reshape(shards * CAP, length, width)[owner_of * CAP + slot_rank]
    negative_coded = encode(negative_hidden, transform_weight)
    passages = jnp.concatenate(
        [positive_coded[:, None], negative_coded.reshape(queries_dev, negatives, length, width)],
        axis=1,
    )
    passages = passages.reshape(queries_dev * (1 + negatives), length, width)
    passage_pool = pooler(lax.all_gather(passages, "shard", axis=0, tiled=True), jnp.int32(0))
    passage_pool = passage_pool.reshape(shards * queries_dev, 1 + negatives, -1)
    pair_terms = jnp.einsum("qv,qjv->qj", query_pool, passage_pool, precision=lax.Precision.HIGHEST)
    sparse = lax.psum_scatter(pair_terms, "shard", scatter_dimension=0, tiled=True) / math.sqrt(
        vocab_total
    )
    inv_root = 1.0 / math.sqrt(width)
    query_cls = query_hidden[:, 0, :]
    positive_cls = positive_hidden[:, 0, :]
    negative_cls = negative_hidden[:, 0, :].reshape(queries_dev, negatives, width)
    query_vec = jnp.dot(query_cls, dense_weight, preferred_element_type=jnp.float32)
    positive_vec = jnp.dot(positive_cls, dense_weight, preferred_element_type=jnp.float32)
    negative_vec = jnp.dot(negative_cls, dense_weight, preferred_element_type=jnp.float32)
    dense_pos = jnp.sum(query_vec * positive_vec, axis=1) * inv_root
    dense_neg = (
        jnp.einsum("qd,qkd->qk", query_vec, negative_vec, precision=lax.Precision.HIGHEST)
        * inv_root
    )
    pos_score = sparse[:, 0] + dense_pos
    neg_score = sparse[:, 1:] + dense_neg
    margin = pos_score[:, None] - neg_score
    target = teacher_margins.astype(jnp.float32) / 1024.0
    coef = (margin - target) / negatives
    coef_total = jnp.sum(coef, axis=1)
    grad_query = (
        coef_total[:, None] * positive_vec
        - jnp.einsum("qk,qkd->qd", coef, negative_vec, precision=lax.Precision.HIGHEST)
    ) * inv_root
    grad_positive = coef_total[:, None] * query_vec * inv_root
    grad_negative = -coef[:, :, None] * query_vec[:, None, :] * inv_root
    states = jnp.concatenate(
        [query_cls, positive_cls, negative_cls.reshape(-1, width)], axis=0
    ).astype(jnp.float32)
    factors = jnp.concatenate([grad_query, grad_positive, grad_negative.reshape(-1, width)], axis=0)
    empty = jnp.zeros((width, width), jnp.float32)
    dense_grad = add_outer(
        empty,
        (
            lax.all_gather(states, ("group", "shard"), axis=0, tiled=True),
            lax.all_gather(factors, ("group", "shard"), axis=0, tiled=True),
        ),
    )
    return (margin, dense_grad)


def solution(mesh):
    in_specs = (
        P(("group", "shard"), None, None),
        P(("group", "shard"), None, None),
        P("shard", None, None),
        P(("group", "shard"), None),
        P(("group", "shard"), None),
        P(),
        P(None, "shard"),
        P(),
    )
    out_specs = (P(("group", "shard"), None), P())
    return jax.shard_map(body, mesh=mesh, in_specs=in_specs, out_specs=out_specs, check_vma=False)
```

profile of v0, /device:TPU:0, one launch (start us, length us, event | category | flops | bytes accessed | tf_op | source)
XLA Modules:
  0.0 263.6 jit_solution(15380211158896153419)
XLA Ops:
  8.6 9.7 %all_to_all.11 = s32[8,1,2]{2,1,0:T(1,128)S(1)} all-to-all(s32[8,1,2]{2,1,0:T(1,128)S(1)} %copy.29), channel_id=1, replica_groups=mesh['group'=4,'shard'=8] {'shard'}, dimensions={0} | all-to-all | bytes 128 | tf_op jit(solution)/shard_map/all_to_all | solution.py:63
  18.6 1.8 gather_fusion
  20.4 2.7 %broadcast_select_fusion = bf16[8,2,64,768]{3,2,1,0:T(8,128)(2,1)} fusion(bf16[8,2,64,768]{3,2,1,0:T(8,128)(2,1)} %bitcast.160, pred[8,2]{1,0:T(8,128)(4,1)S(1)} %copy.31), kind=kLoop, calls=%fused_computation.37 | loop fusion | flops 786432 | bytes 3145744 | tf_op jit(solution)/shard_map/jit(_where)/select_n | solution.py:66
  23.1 4.4 %all-to-all-start.1 = ((bf16[8,2,64,768]{3,2,1,0:T(8,128)(2,1)}), bf16[8,2,64,768]{3,2,1,0:T(8,128)(2,1)}, u32[]{:S(2)}, u32[]{:S(2)}) async-start(bf16[8,2,64,768]{3,2,1,0:T(8,128)(2,1)} %broadcast_select_fusion), calls=%async_computation.1 | async-start | bytes 3145728 | tf_op jit(solution)/shard_map/all_to_all | solution.py:67
  27.7 2.0 fusion.77
  30.0 18.5 %all-to-all-done.1 = bf16[8,2,64,768]{3,2,1,0:T(8,128)(2,1)} async-done(((bf16[8,2,64,768]{3,2,1,0:T(8,128)(2,1)}), bf16[8,2,64,768]{3,2,1,0:T(8,128)(2,1)}, u32[]{:S(2)}, u32[]{:S(2)}) %all-to-all-start.1) | async-done | bytes 1572896 | tf_op jit(solution)/shard_map/all_to_all | solution.py:67
  48.6 2.9 %gather_fusion.1 = bf16[8,64,768]{2,1,0:T(8,128)(2,1)} fusion(bf16[16,64,768]{2,1,0:T(8,128)(2,1)} %bitcast.14, s32[1024]{0:T(1024)S(1)} %pad_clamp_fusion), kind=kCustom, calls=%fused_computation.1 | custom fusion | bytes 1572896 | tf_op jit(solution)/shard_map/gather | solution.py:68
  51.4 2.8 %fusion.31 = (u8[64,768]{1,0:T(8,128)(4,1)S(1)}, u8[64,768]{1,0:T(8,128)(4,1)S(1)}, u8[64,768]{1,0:T(8,128)(4,1)S(1)}, f32[8,64,768]{2,1,0:T(8,128)S(1)}) fusion(bf16[8,64,768]{2,1,0:T(8,128)(2,1)} %gather_fusion.1, bf16[768,768]{1,0:T(8,128)(2,1)} %param.15), kind=kOutput, calls=%fused_computation.51 | convolution fusion | flops 611696640 | bytes 3686400 | tf_op jit(solution)/shard_map/dot_general | solution.py:13
  54.3 3.8 %fusion.75 = (f32[8,64]{1,0:T(8,128)S(1)}, f32[8,64,768]{2,1,0:T(8,128)S(1)}) fusion(u8[64,768]{1,0:T(8,128)(4,1)S(1)} %get-tuple-element.38, u8[64,768]{1,0:T(8,128)(4,1)S(1)} %get-tuple-element.39, f32[8,64,768]{2,1,0:T(8,128)S(1)} %get-tuple-element.56, u8[64,768]{1,0:T(8,128)(4,1)S(1)} %get-tuple-element.37), kind=kLoop, calls=%fused_computation.154 | loop fusion | flops 28311040 | bytes 3295232 | tf_op jit(solution)/shard_map/reduce_sum | solution.py:15
  60.4 1.6 convolution_reduce_fusion.1
  62.0 1.6 fusion.79
  64.9 2.1 fusion.78
  67.3 10.4 %all-gather = bf16[256,768]{1,0:T(8,128)(2,1)S(1)} all-gather(bf16[32,768]{1,0:T(8,128)(2,1)S(1)} %multiply_convert_fusion.2), channel_id=2, replica_groups=mesh['group'=4,'shard'=8] {'shard'}, dimensions={0}, use_global_device_ids=true | all-gather | bytes 442368 | tf_op jit(solution)/shard_map/all_gather | solution.py:50
  80.1 50.6 %all-gather.2 = f32[32,10,768]{2,1,0:T(8,128)} all-gather(f32[1,10,768]{2,1,0:T(8,128)S(1)} %fusion.62), channel_id=1, replica_groups=mesh['group'=4,'shard'=8] {'group','shard'}, dimensions={0}, use_global_device_ids=true | all-gather | bytes 1013760 | tf_op jit(solution)/shard_map/all_gather | solution.py:113
  130.8 2.5 reshape.544
  133.3 1.5 fusion.80
  134.8 48.1 %while.2 = (s32[]{:T(128)}, f32[9,8,1920]{2,1,0:T(8,128)}, bf16[9,8,64,768]{3,2,1,0:T(8,128)(2,1)}, bf16[768,1920]{1,0:T(8,128)(2,1)}, s32[]{:T(128)}) while((s32[]{:T(128)}, f32[9,8,1920]{2,1,0:T(8,128)}, bf16[9,8,64,768]{3,2,1,0:T(8,128)(2,1)}, bf16[768,1920]{1,0:T(8,128)(2,1)}, s32[]{:T(128)}) %tuple.40), condition=%wide.region_13.14_spmd, body=%wide.region_11.13_spmd.sunk | while | flops 1511900160 | bytes 3919949 | solution.py:26
  134.8 4.7 %log-plus-one_reduce_fusion.2 = f32[8,1920]{1,0:T(8,128)S(1)} fusion(bf16[768,1920]{1,0:T(8,128)(2,1)} %get-tuple-element.102, bf16[9,8,64,768]{3,2,1,0:T(8,128)(2,1)} %get-tuple-element.101, s32[]{:T(128)S(6)} %copy.45), kind=kOutput, calls=%fused_computation.2.clone.1 | convolution fusion | flops 1511900160 | bytes 3796996 | tf_op jit(solution)/shard_map/while/body/eval_jaxpr/vmap()/dot_general | solution.py:21
  140.2 4.7 %log-plus-one_reduce_fusion.2 = f32[8,1920]{1,0:T(8,128)S(1)} fusion(bf16[768,1920]{1,0:T(8,128)(2,1)} %get-tuple-element.102, bf16[9,8,64,768]{3,2,1,0:T(8,128)(2,1)} %get-tuple-element.101, s32[]{:T(128)S(6)} %copy.45), kind=kOutput, calls=%fused_computation.2.clone.1 | convolution fusion | flops 1511900160 | bytes 3796996 | tf_op jit(solution)/shard_map/while/body/eval_jaxpr/vmap()/dot_general | solution.py:21
  145.5 4.7 %log-plus-one_reduce_fusion.2 = f32[8,1920]{1,0:T(8,128)S(1)} fusion(bf16[768,1920]{1,0:T(8,128)(2,1)} %get-tuple-element.102, bf16[9,8,64,768]{3,2,1,0:T(8,128)(2,1)} %get-tuple-element.101, s32[]{:T(128)S(6)} %copy.45), kind=kOutput, calls=%fused_computation.2.clone.1 | convolution fusion | flops 1511900160 | bytes 3796996 | tf_op jit(solution)/shard_map/while/body/eval_jaxpr/vmap()/dot_general | solution.py:21
  150.9 4.7 %log-plus-one_reduce_fusion.2 = f32[8,1920]{1,0:T(8,128)S(1)} fusion(bf16[768,1920]{1,0:T(8,128)(2,1)} %get-tuple-element.102, bf16[9,8,64,768]{3,2,1,0:T(8,128)(2,1)} %get-tuple-element.101, s32[]{:T(128)S(6)} %copy.45), kind=kOutput, calls=%fused_computation.2.clone.1 | convolution fusion | flops 1511900160 | bytes 3796996 | tf_op jit(solution)/shard_map/while/body/eval_jaxpr/vmap()/dot_general | solution.py:21
  156.2 4.7 %log-plus-one_reduce_fusion.2 = f32[8,1920]{1,0:T(8,128)S(1)} fusion(bf16[768,1920]{1,0:T(8,128)(2,1)} %get-tuple-element.102, bf16[9,8,64,768]{3,2,1,0:T(8,128)(2,1)} %get-tuple-element.101, s32[]{:T(128)S(6)} %copy.45), kind=kOutput, calls=%fused_computation.2.clone.1 | convolution fusion | flops 1511900160 | bytes 3796996 | tf_op jit(solution)/shard_map/while/body/eval_jaxpr/vmap()/dot_general | solution.py:21
  161.6 4.7 %log-plus-one_reduce_fusion.2 = f32[8,1920]{1,0:T(8,128)S(1)} fusion(bf16[768,1920]{1,0:T(8,128)(2,1)} %get-tuple-element.102, bf16[9,8,64,768]{3,2,1,0:T(8,128)(2,1)} %get-tuple-element.101, s32[]{:T(128)S(6)} %copy.45), kind=kOutput, calls=%fused_computation.2.clone.1 | convolution fusion | flops 1511900160 | bytes 3796996 | tf_op jit(solution)/shard_map/while/body/eval_jaxpr/vmap()/dot_general | solution.py:21
  166.9 4.7 %log-plus-one_reduce_fusion.2 = f32[8,1920]{1,0:T(8,128)S(1)} fusion(bf16[768,1920]{1,0:T(8,128)(2,1)} %get-tuple-element.102, bf16[9,8,64,768]{3,2,1,0:T(8,128)(2,1)} %get-tuple-element.101, s32[]{:T(128)S(6)} %copy.45), kind=kOutput, calls=%fused_computation.2.clone.1 | convolution fusion | flops 1511900160 | bytes 3796996 | tf_op jit(solution)/shard_map/while/body/eval_jaxpr/vmap()/dot_general | solution.py:21
  172.3 4.7 %log-plus-one_reduce_fusion.2 = f32[8,1920]{1,0:T(8,128)S(1)} fusion(bf16[768,1920]{1,0:T(8,128)(2,1)} %get-tuple-element.102, bf16[9,8,64,768]{3,2,1,0:T(8,128)(2,1)} %get-tuple-element.101, s32[]{:T(128)S(6)} %copy.45), kind=kOutput, calls=%fused_computation.2.clone.1 | convolution fusion | flops 1511900160 | bytes 3796996 | tf_op jit(solution)/shard_map/while/body/eval_jaxpr/vmap()/dot_general | solution.py:21
  177.6 4.7 %log-plus-one_reduce_fusion.2 = f32[8,1920]{1,0:T(8,128)S(1)} fusion(bf16[768,1920]{1,0:T(8,128)(2,1)} %get-tuple-element.102, bf16[9,8,64,768]{3,2,1,0:T(8,128)(2,1)} %get-tuple-element.101, s32[]{:T(128)S(6)} %copy.45), kind=kOutput, calls=%fused_computation.2.clone.1 | convolution fusion | flops 1511900160 | bytes 3796996 | tf_op jit(solution)/shard_map/while/body/eval_jaxpr/vmap()/dot_general | solution.py:21
  182.9 2.1 reshape_reshape.3
  185.0 2.5 fusion.56
  187.5 12.1 %all-reduce = f32[8,9]{1,0:T(8,128)S(1)} all-reduce(f32[8,9]{1,0:T(8,128)S(1)} %bitcast.165), channel_id=4, replica_groups=mesh['group'=4,'shard'=8] {'shard'}, use_global_device_ids=true, to_apply=%region_14.15.clone | all-reduce | flops 72 | bytes 576
  203.4 44.1 %all-gather.3 = f32[32,10,768]{2,1,0:T(8,128)} all-gather(f32[1,10,768]{2,1,0:T(8,128)S(1)} %maximum_bitcast_fusion.1), channel_id=1, replica_groups=mesh['group'=4,'shard'=8] {'group','shard'}, dimensions={0}, use_global_device_ids=true | all-gather | bytes 1013760 | tf_op jit(solution)/shard_map/all_gather | solution.py:114
  247.5 2.4 reshape.546
  249.9 6.9 %fusion.81 = f32[768,768]{1,0:T(8,128)} fusion(f32[320,768]{1,0:T(8,128)} %reshape.544, f32[320,768]{1,0:T(8,128)} %reshape.546), kind=kOutput, calls=%fused_computation.159 | convolution fusion | flops 2264924160 | bytes 4325376 | tf_op jit(solution)/shard_map/rd,re->de/dot_general | solution.py:30
  (76 shorter events, 17.0 us)
Async XLA Ops:
  7.2 11.4 %copy-start = (bf16[32,64,768]{2,1,0:T(8,128)(2,1)S(1)}, bf16[32,64,768]{2,1,0:T(8,128)(2,1)}, u32[]{:S(2)}) copy-start(bf16[32,64,768]{2,1,0:T(8,128)(2,1)} %param.12) | copy-start | bytes 9437188
  23.1 4.5 %copy-start.5 = (s32[1,8]{1,0:T(1,128)S(1)}, s32[1,8]{1,0:T(1,128)}, u32[]{:S(2)}) copy-start(s32[1,8]{1,0:T(1,128)} %param.13) | copy-start | bytes 100
  23.1 4.5 %copy-start.2 = (bf16[1,64,768]{2,1,0:T(8,128)(2,1)S(1)}, bf16[1,64,768]{2,1,0:T(8,128)(2,1)}, u32[]{:S(2)}) copy-start(bf16[1,64,768]{2,1,0:T(8,128)(2,1)} %param.11) | copy-start | bytes 294916
  23.1 25.4 %all-to-all-start.1 = ((bf16[8,2,64,768]{3,2,1,0:T(8,128)(2,1)}), bf16[8,2,64,768]{3,2,1,0:T(8,128)(2,1)}, u32[]{:S(2)}, u32[]{:S(2)}) async-start(bf16[8,2,64,768]{3,2,1,0:T(8,128)(2,1)} %broadcast_select_fusion), calls=%async_computation.1 | async-start | bytes 3145728 | tf_op jit(solution)/shard_map/all_to_all | solution.py:67
  27.6 107.3 %all-gather.6.cloned.1.call-start = ((), (), s32[]{:S(2)}) async-start(), calls=%async_computation.2 | async-start | bytes 7962624 | tf_op jit(solution)/shard_map/all_gather | solution.py:75
  58.7 1.1 copy-start.6
  58.7 3.3 %copy-start.1 = (bf16[1,32,768]{2,1,0:T(8,128)(2,1)S(1)}, bf16[1,32,768]{2,1,0:T(8,128)(2,1)}, u32[]{:S(2)}) copy-start(bf16[1,32,768]{2,1,0:T(8,128)(2,1)} %param.10) | copy-start | bytes 147460
  64.9 12.8 %copy-start.4 = (bf16[768,1920]{1,0:T(8,128)(2,1)S(1)}, bf16[768,1920]{1,0:T(8,128)(2,1)}, u32[]{:S(2)}) copy-start(bf16[768,1920]{1,0:T(8,128)(2,1)} %param.16) | copy-start | bytes 8847364
  182.9 17.4 %copy-start.3 = (s32[1,8]{1,0:T(1,128)S(1)}, s32[1,8]{1,0:T(1,128)}, u32[]{:S(2)}) copy-start(s32[1,8]{1,0:T(1,128)} %param.14) | copy-start | bytes 100
Sparse Core Ops, SparseCore 0:
  59.9 59.8 all-gather.5
where the time goes:
time: 264 us
  blocking collectives  127 us (48%)
  matrix products  66.2 us (25%)
  local copies, waits for them, and re-layouts  19.4 us (7%)
  waiting for transfers between devices  18.6 us (7%)
  between operations  15.1 us (6%)
  other arithmetic  12.9 us (5%)
  starting transfers between devices  4.46 us (2%)
    all_gather x1, blocking collectives, body(): lax.all_gather(states, ('group', 'shard'), axis=0, tiled=True)  50.6 us
    all_gather x1, blocking collectives, body(): lax.all_gather(factors, ('group', 'shard'), axis=0, tiled=True)  44.1 us
    dot_general x10, matrix products, pool_single(): logits = jnp.dot(sequence, vocab_weight, preferred_element_type=jnp.float32)  43.8 us
    all_to_all x1, waiting for transfers between devices, body(): lax.all_to_all(served, 'shard', split_axis=0, concat_axis=0, tiled=True)  18.5 us
    unnamed x1, blocking collectives  12.1 us
    all_gather x1, blocking collectives, body(): lax.all_gather(query_coded, 'shard', axis=0, tiled=True)  10.4 us
    all_to_all x1, blocking collectives, body(): lax.all_to_all(requests, 'shard', split_axis=0, concat_axis=0, tiled=True)  9.68 us
    dot_general x3, matrix products, encode(): jnp.dot(hidden, transform_weight, preferred_element_type=jnp.float32)  6.94 us
  transfers between devices with their start and end apart: 2, of which 1 were waited for; matrix products, arithmetic and copies ran while one was open for 6% of the time, Pallas kernels for 0%

commit v1 on v0

v1 whole, which is shorter than its diff:
```python
import functools
import math

import jax
import jax.numpy as jnp
from jax import lax
from jax.experimental import pallas as pl
from jax.experimental.pallas import tpu as pltpu
from jax.sharding import PartitionSpec as P

LANES = 256
COLS = 512
TILE_ROWS = 512
CHUNK_PASSAGES = 2
HIGHEST = lax.Precision.HIGHEST
MESH_ID = pl.DeviceIdType.MESH


def encode(hidden, transform_weight):
    mixed = jnp.dot(hidden, transform_weight, preferred_element_type=jnp.float32)
    active = 0.5 * mixed * (1.0 + lax.erf(mixed * math.sqrt(0.5)))
    centre = jnp.mean(active, axis=-1, keepdims=True)
    shifted = active - centre
    spread = jnp.mean(shifted * shifted, axis=-1, keepdims=True)
    return (shifted * lax.rsqrt(spread + 1e-05)).astype(jnp.bfloat16)


def exchange_kernel(
    groups,
    shards,
    lq,
    query_ref,
    positive_ref,
    cls_ref,
    meta_ref,
    transform_ref,
    store_ref,
    vocab_ref,
    tables_out,
    cls_out,
    meta_out,
    hidden,
    vocab,
    cls_buf,
    meta_buf,
    front,
    coded,
    query_pool,
    passage_pool,
    partial,
    tables,
    load_sem,
    tree_send,
    tree_recv,
    meta_send,
    meta_recv,
    pool_send,
    pool_recv,
    part_send,
    part_recv,
    table_send,
    table_recv,
):
    group = lax.axis_index("group")
    shard = lax.axis_index("shard")
    devices = groups * shards
    linear = group * shards + shard
    bits = shards.bit_length() - 1
    queries, lp, width = positive_ref.shape
    chunks, _, chunk_rows, _ = coded.shape
    chunk_passages = chunk_rows // lp
    share = chunks * chunk_passages
    columns = vocab.shape[1]
    front_query = queries * lq
    store_total = share * shards

    digit = [(shard // (1 << i)) % 2 for i in range(bits)]

    def partner(offset):
        index = 0
        for i in range(bits):
            index = index + ((1 - digit[i]) if (offset >> i) & 1 else digit[i]) * (1 << i)
        return index

    peers = [partner(offset) for offset in range(shards)]

    load_store = pltpu.make_async_copy(
        store_ref.at[pl.ds(group * share, share)], hidden, load_sem.at[0]
    )
    load_vocab = pltpu.make_async_copy(vocab_ref, vocab, load_sem.at[1])
    load_store.start()
    load_vocab.start()

    barrier = pltpu.get_barrier_semaphore()

    def greet(i, carry):
        other = (linear + i) % devices
        pl.semaphore_signal(
            barrier, inc=1, device_id=(other // shards, other % shards), device_id_type=MESH_ID
        )
        return carry

    lax.fori_loop(1, devices, greet, 0)

    def block(chunk, slot):
        if chunk == 0:
            return cls_buf.at[slot]
        if chunk == 1:
            return front.at[slot]
        return coded.at[chunk - 2, slot]

    def order(chunk):
        outer = list(range(1, bits))
        return (outer if chunk % 2 == 0 else outer[::-1]) + [0]

    def hop(chunk, offset, dim):
        source = cls_ref if chunk == 0 and offset == 0 else block(chunk, peers[offset])
        return pltpu.make_async_remote_copy(
            src_ref=source,
            dst_ref=block(chunk, peers[offset]),
            send_sem=tree_send.at[chunk, offset, dim],
            recv_sem=tree_recv.at[chunk, offset ^ (1 << dim)],
            device_id={"shard": peers[1 << dim]},
            device_id_type=MESH_ID,
        )

    def arrived(chunk, offset):
        pltpu.make_async_remote_copy(
            src_ref=block(chunk, peers[offset]),
            dst_ref=block(chunk, peers[offset]),
            send_sem=tree_send.at[chunk, 0, 0],
            recv_sem=tree_recv.at[chunk, offset],
            device_id={"shard": peers[1]},
            device_id_type=MESH_ID,
        ).wait_recv()

    hops = []

    def forward(chunk, offset):
        path = order(chunk)
        last = max([path.index(i) for i in range(bits) if (offset >> i) & 1], default=-1)
        for dim in path[last + 1 :]:
            copy = hop(chunk, offset, dim)
            copy.start()
            hops.append(copy)

    def relay(chunk, level):
        for offset in range(0, shards, 2):
            if offset.bit_count() == level:
                arrived(chunk, offset)
                forward(chunk, offset)

    def finish(chunk):
        for offset in range(1, shards, 2):
            arrived(chunk, offset)

    def encode_chunk(chunk):
        if chunk == 1:
            rows = jnp.concatenate(
                [
                    query_ref[...].reshape(front_query, width),
                    positive_ref[...].reshape(queries * lp, width),
                ],
                axis=0,
            )
            front[shard] = encode(rows, transform_ref[...])
        else:
            first = (chunk - 2) * chunk_passages
            rows = hidden[first : first + chunk_passages].reshape(chunk_rows, width)
            coded[chunk - 2, shard] = encode(rows, transform_ref[...])

    def pool(rows, length, target):
        sequences = rows.shape[0] // length
        for start in range(0, columns, COLS):
            stop = min(start + COLS, columns)
            logits = jnp.dot(rows, vocab[:, start:stop], preferred_element_type=jnp.float32)
            best = jnp.max(logits.reshape(sequences, length, stop - start), axis=1)
            target(start, stop, jnp.log1p(jnp.maximum(best, 0.0)))

    def pool_front():
        def put_query(start, stop, values):
            query_pool[group, :, start:stop] = values

        def put_positive(start, stop, values):
            passage_pool[store_total : store_total + shards * queries, start:stop] = values

        pool(front[:, :front_query].reshape(shards * front_query, width), lq, put_query)
        for i in range(1, groups):
            send_pool(i).start()
        pool(front[:, front_query:].reshape(shards * queries * lp, width), lp, put_positive)

    slots = max(1, min(shards, TILE_ROWS // chunk_rows))

    def pool_chunk(chunk):
        def step(i, carry):
            rows = coded[chunk - 2, pl.ds(i * slots, slots)].reshape(slots * chunk_rows, width)
            tall = slots * chunk_passages
            base = (chunk - 2) * shards * chunk_passages + i * tall

            def put(start, stop, values):
                passage_pool[pl.ds(pl.multiple_of(base, tall), tall), start:stop] = values

            pool(rows, lp, put)
            return carry

        lax.fori_loop(0, shards // slots, step, 0)

    def send_pool(i):
        return pltpu.make_async_remote_copy(
            src_ref=query_pool.at[group],
            dst_ref=query_pool.at[group],
            send_sem=pool_send.at[i],
            recv_sem=pool_recv.at[i],
            device_id={"group": (group + i) % groups},
            device_id_type=MESH_ID,
        )

    def pool_arrived(i):
        slot = (group + groups - i) % groups
        pltpu.make_async_remote_copy(
            src_ref=query_pool.at[slot],
            dst_ref=query_pool.at[slot],
            send_sem=pool_send.at[i],
            recv_sem=pool_recv.at[i],
            device_id={"group": (group + i) % groups},
            device_id_type=MESH_ID,
        ).wait_recv()

    def meta_copy(i, sender):
        other = (linear + i) % devices
        return pltpu.make_async_remote_copy(
            src_ref=meta_ref,
            dst_ref=meta_buf.at[sender],
            send_sem=meta_send.at[i],
            recv_sem=meta_recv.at[i],
            device_id=(other // shards, other % shards),
            device_id_type=MESH_ID,
        )

    encode_chunk(1)
    cls_buf[shard] = cls_ref[...]
    meta_buf[linear] = meta_ref[...]
    passage_pool[store_total + shards * queries :, :] = jnp.zeros(
        (passage_pool.shape[0] - store_total - shards * queries, columns), jnp.float32
    )
    pl.semaphore_wait(barrier, devices - 1)

    total = chunks + 2
    for step in range(total + bits - 1):
        if step < total:
            if step == 2:
                load_store.wait()
            if step >= 2:
                encode_chunk(step)
            forward(step, 0)
            if step == 1:

                def send_meta(i, carry):
                    meta_copy(i, linear).start()
                    return carry

                lax.fori_loop(1, devices, send_meta, 0)
        for level in range(1, bits):
            if 0 <= step - level < total:
                relay(step - level, level)
        ready = step - bits + 1
        if 0 <= ready < total:
            finish(ready)
            if ready == 1:
                load_vocab.wait()
                pool_front()
            elif ready > 1:
                pool_chunk(ready)

    for i in range(1, groups):
        pool_arrived(i)
    stacked = query_pool[...].reshape(groups * shards * queries, columns)
    partial[shard] = lax.dot_general(
        stacked,
        passage_pool[...],
        (((1,), (1,)), ((), ())),
        precision=HIGHEST,
        preferred_element_type=jnp.float32,
    )

    def part_copy(offset, slot):
        return pltpu.make_async_remote_copy(
            src_ref=partial.at[slot],
            dst_ref=partial.at[slot],
            send_sem=part_send.at[offset],
            recv_sem=part_recv.at[offset],
            device_id={"shard": peers[offset]},
            device_id_type=MESH_ID,
        )

    for offset in range(1, shards):
        part_copy(offset, shard).start()
    for offset in range(1, shards):
        part_copy(offset, peers[offset]).wait_recv()
    tables[group] = jnp.sum(partial[...], axis=0)

    def table_copy(i, slot):
        return pltpu.make_async_remote_copy(
            src_ref=tables.at[slot],
            dst_ref=tables.at[slot],
            send_sem=table_send.at[i],
            recv_sem=table_recv.at[i],
            device_id={"group": (group + i) % groups},
            device_id_type=MESH_ID,
        )

    for i in range(1, groups):
        table_copy(i, group).start()

    def meta_arrived(i, carry):
        meta_copy(i, (linear + devices - i) % devices).wait_recv()
        return carry

    lax.fori_loop(1, devices, meta_arrived, 0)
    cls_out[...] = cls_buf[...]
    meta_out[...] = meta_buf[...]

    def meta_sent(i, carry):
        meta_copy(i, linear).wait_send()
        return carry

    lax.fori_loop(1, devices, meta_sent, 0)
    for copy in hops:
        copy.wait_send()
    for i in range(1, groups):
        send_pool(i).wait_send()
    for offset in range(1, shards):
        part_copy(offset, shard).wait_send()
    for i in range(1, groups):
        table_copy(i, (group + groups - i) % groups).wait_recv()
    tables_out[...] = tables[...]
    for i in range(1, groups):
        table_copy(i, group).wait_send()


def dot(left, right, dims):
    return lax.dot_general(
        left, right, (dims, ((), ())), precision=HIGHEST, preferred_element_type=jnp.float32
    )


def split_dot(left, right):
    high = right.astype(jnp.bfloat16)
    rest = right - high.astype(jnp.float32)
    low = rest.astype(jnp.bfloat16)
    dims = (((0,), (0,)), ((), ()))
    return lax.dot_general(
        left, high, dims, preferred_element_type=jnp.float32
    ) + lax.dot_general(left, low, dims, preferred_element_type=jnp.float32)


def loss_kernel(
    groups,
    shards,
    negatives,
    chunk_passages,
    vocab_total,
    tables_ref,
    cls_ref,
    meta_ref,
    dense_ref,
    margin_ref,
    grad_ref,
    margin_buf,
):
    _, store_rows, width = cls_ref.shape
    total, _, lanes = meta_ref.shape
    passages = shards * store_rows
    own = margin_ref.shape[0]
    share = store_rows // groups
    chunks = share // chunk_passages
    parts = width // lanes
    table_cols = tables_ref.shape[2]
    inv_root = 1.0 / math.sqrt(width)
    inv_vocab = 1.0 / math.sqrt(vocab_total)
    query_cls = jnp.concatenate([meta_ref[:, i, :] for i in range(parts)], axis=1).astype(
        jnp.bfloat16
    )
    positive_cls = jnp.concatenate(
        [meta_ref[:, parts + i, :] for i in range(parts)], axis=1
    ).astype(jnp.bfloat16)
    labels = meta_ref[:, 2 * parts, :]
    ids = labels[:, :negatives].astype(jnp.int32)
    targets = labels[:, negatives : 2 * negatives] / 1024.0
    store_cls = cls_ref[...].reshape(passages, width)
    dense = dense_ref[...]
    query_vec = jnp.dot(query_cls, dense, preferred_element_type=jnp.float32)
    positive_vec = jnp.dot(positive_cls, dense, preferred_element_type=jnp.float32)
    store_vec = jnp.dot(store_cls, dense, preferred_element_type=jnp.float32)
    dense_pos = jnp.sum(query_vec * positive_vec, axis=1, keepdims=True) * inv_root
    dense_all = dot(query_vec, store_vec, ((1,), (1,))) * inv_root

    row = lax.broadcasted_iota(jnp.int32, (total, table_cols), 0)
    column = lax.broadcasted_iota(jnp.int32, (total, table_cols), 1)
    span = total // groups
    sparse_pos = jnp.zeros((total, 1), jnp.float32)
    for g in range(groups):
        hit = (row - g * span) == (column - share * shards)
        hit = hit & (column >= share * shards) & (row >= g * span) & (row < (g + 1) * span)
        sparse_pos = sparse_pos + jnp.sum(
            jnp.where(hit, tables_ref[g], 0.0), axis=1, keepdims=True
        )
    pos_score = sparse_pos * inv_vocab + dense_pos

    passage = lax.broadcasted_iota(jnp.int32, (total, passages), 1)
    weights = jnp.zeros((total, passages), jnp.float32)
    coef_total = jnp.zeros((total, 1), jnp.float32)
    margins = jnp.zeros((total, table_cols), jnp.float32)
    for k in range(negatives):
        number = ids[:, k : k + 1]
        owner = number // store_rows
        local = number - owner * store_rows
        part = local // share
        inner = local - part * share
        chunk = inner // chunk_passages
        place = (chunk * shards + owner) * chunk_passages + inner - chunk * chunk_passages
        here = column == place
        sparse_neg = jnp.zeros((total, 1), jnp.float32)
        for g in range(groups):
            sparse_neg = sparse_neg + jnp.sum(
                jnp.where(here & (part == g), tables_ref[g], 0.0), axis=1, keepdims=True
            )
        named = passage == number
        dense_neg = jnp.sum(jnp.where(named, dense_all, 0.0), axis=1, keepdims=True)
        margin = pos_score - (sparse_neg * inv_vocab + dense_neg)
        coef = (margin - targets[:, k : k + 1]) / negatives
        weights = weights + jnp.where(named, coef, 0.0)
        coef_total = coef_total + coef
        margins = jnp.where(column == k, margin, margins)
    margin_buf[...] = margins
    linear = lax.axis_index("group") * shards + lax.axis_index("shard")
    margin_ref[...] = margin_buf[pl.ds(linear * own, own), :negatives]

    grad_query = (coef_total * positive_vec - dot(weights, store_vec, ((1,), (0,)))) * inv_root
    grad_positive = coef_total * query_vec * inv_root
    grad_store = dot(weights, query_vec, ((0,), (0,))) * (-inv_root)
    states = jnp.concatenate([query_cls, positive_cls, store_cls], axis=0)
    factors = jnp.concatenate([grad_query, grad_positive, grad_store], axis=0)
    grad_ref[...] = split_dot(states, factors)


def body(
    query_hidden,
    positive_hidden,
    passage_store,
    negative_ids,
    teacher_margins,
    transform_weight,
    vocab_weight,
    dense_weight,
):
    groups = lax.axis_size("group")
    shards = lax.axis_size("shard")
    devices = groups * shards
    bits = shards.bit_length() - 1
    queries, lq, width = query_hidden.shape
    store_rows, lp, _ = passage_store.shape
    negatives = negative_ids.shape[1]
    columns = vocab_weight.shape[1]
    share = store_rows // groups
    chunk_passages = min(CHUNK_PASSAGES, share)
    chunks = share // chunk_passages
    parts = width // LANES
    rows = 2 * parts + 1
    rows += -rows % 8
    pooled = share * shards + shards * queries
    pooled += -pooled % 128
    total = devices * queries

    labels = jnp.concatenate([negative_ids, teacher_margins], axis=1).astype(jnp.float32)
    labels = jnp.pad(labels, ((0, 0), (0, LANES - 2 * negatives)))
    meta = jnp.concatenate(
        [
            query_hidden[:, 0, :].astype(jnp.float32).reshape(queries, parts, LANES),
            positive_hidden[:, 0, :].astype(jnp.float32).reshape(queries, parts, LANES),
            labels[:, None, :],
            jnp.zeros((queries, rows - 2 * parts - 1, LANES), jnp.float32),
        ],
        axis=1,
    )
    store_cls = passage_store[:, 0, :]

    vmem = pl.BlockSpec(memory_space=pltpu.VMEM)
    hbm = pl.BlockSpec(memory_space=pl.ANY)
    dma = pltpu.SemaphoreType.DMA
    tables, cls_all, meta_all = pl.pallas_call(
        functools.partial(exchange_kernel, groups, shards, lq),
        out_shape=[
            jax.ShapeDtypeStruct((groups, total, pooled), jnp.float32),
            jax.ShapeDtypeStruct((shards, store_rows, width), jnp.bfloat16),
            jax.ShapeDtypeStruct((devices, queries, rows, LANES), jnp.float32),
        ],
        in_specs=[vmem] * 5 + [hbm] * 2,
        out_specs=[vmem] * 3,
        scratch_shapes=[
            pltpu.VMEM((share, lp, width), jnp.bfloat16),
            pltpu.VMEM((width, columns), jnp.bfloat16),
            pltpu.VMEM((shards, store_rows, width), jnp.bfloat16),
            pltpu.VMEM((devices, queries, rows, LANES), jnp.float32),
            pltpu.VMEM((shards, queries * (lq + lp), width), jnp.bfloat16),
            pltpu.VMEM((chunks, shards, chunk_passages * lp, width), jnp.bfloat16),
            pltpu.VMEM((groups, shards * queries, columns), jnp.float32),
            pltpu.VMEM((pooled, columns), jnp.float32),
            pltpu.VMEM((shards, total, pooled), jnp.float32),
            pltpu.VMEM((groups, total, pooled), jnp.float32),
            dma((2,)),
            dma((chunks + 2, shards, bits)),
            dma((chunks + 2, shards)),
            dma((devices,)),
            dma((devices,)),
            dma((groups,)),
            dma((groups,)),
            dma((shards,)),
            dma((shards,)),
            dma((groups,)),
            dma((groups,)),
        ],
        compiler_params=pltpu.CompilerParams(
            collective_id=0, has_side_effects=True, vmem_limit_bytes=56 * 1024 * 1024
        ),
        name="exchange",
    )(
        query_hidden,
        positive_hidden,
        store_cls,
        meta,
        transform_weight,
        passage_store,
        vocab_weight,
    )
    return pl.pallas_call(
        functools.partial(
            loss_kernel, groups, shards, negatives, chunk_passages, columns * shards
        ),
        out_shape=[
            jax.ShapeDtypeStruct((queries, negatives), jnp.float32),
            jax.ShapeDtypeStruct((width, width), jnp.float32),
        ],
        in_specs=[vmem] * 4,
        out_specs=[vmem] * 2,
        scratch_shapes=[pltpu.VMEM((total, pooled), jnp.float32)],
        compiler_params=pltpu.CompilerParams(vmem_limit_bytes=32 * 1024 * 1024),
        name="loss",
    )(tables, cls_all, meta_all.reshape(total, rows, LANES), dense_weight)


def solution(mesh):
    in_specs = (
        P(("group", "shard"), None, None),
        P(("group", "shard"), None, None),
        P("shard", None, None),
        P(("group", "shard"), None),
        P(("group", "shard"), None),
        P(),
        P(None, "shard"),
        P(),
    )
    out_specs = (P(("group", "shard"), None), P())
    return jax.shard_map(body, mesh=mesh, in_specs=in_specs, out_specs=out_specs, check_vma=False)
```

time: 264 us -> 83.6 us (0.32)
  blocking collectives: 127 us -> 0 us
  Pallas kernels: 0 us -> 75.1 us
  matrix products: 66.2 us -> 0 us
  waiting for transfers between devices: 18.6 us -> 0 us
  local copies, waits for them, and re-layouts: 19.4 us -> 4.56 us
  between operations: 15.1 us -> 0.68 us
  other arithmetic: 12.9 us -> 2.85 us
  starting transfers between devices: 4.46 us -> 0 us
    all_gather x3 -> x0, blocking collectives: 105 us -> none  [the longest x1 50.6 us: body(): lax.all_gather(states, ('group', 'shard'), axis=0, tiled=True)]
    pallas_call x0 -> x2, Pallas kernels: none -> 75.1 us  [the longest x1 66.5 us: body(): pl.pallas_call(functools.partial(exchange_kernel, groups, shards, lq), ou...]
    dot_general x20 -> x0, matrix products: 66.2 us -> none  [the longest x10 43.8 us: pool_single(): logits = jnp.dot(sequence, vocab_weight, preferred_element_type=jnp.float32)]
    all_to_all x1 -> x0, waiting for transfers between devices: 18.5 us -> none  [body(): lax.all_to_all(served, 'shard', split_axis=0, concat_axis=0, tiled=True)]
    unnamed x1 -> x0, blocking collectives: 12.1 us -> none
    all_to_all x1 -> x0, blocking collectives: 9.68 us -> none  [body(): lax.all_to_all(requests, 'shard', split_axis=0, concat_axis=0, tiled=True)]
    dynamic_update_slice x9 -> x0, local copies, waits for them, and re-layouts: 5.69 us -> none  [pool_sequences(): lax.map(partial(pool_single, vocab_weight=vocab_weight), block_rows, batc...]
    reduce_sum x7 -> x0, other arithmetic: 5.49 us -> none  [the longest x1 3.84 us: encode(): centre = jnp.mean(active, axis=-1, keepdims=True)]
  transfers between devices with their start and end apart: 2 -> 0, of which waited for: 1 -> 0; matrix products, arithmetic and copies ran while one was open for 6% -> 0% of each run, Pallas kernels for 0% -> 0%
where the time goes in v1:
time: 83.6 us; the launch traced here: 83.2 us
  Pallas kernels  75.1 us (90%)
  local copies, waits for them, and re-layouts  4.56 us (5%)
  other arithmetic  2.85 us (3%)
    pallas_call x1, Pallas kernels, body(): pl.pallas_call(functools.partial(exchange_kernel, groups, shards, lq), ou...  66.5 us
    pallas_call x1, Pallas kernels, body(): pl.pallas_call(functools.partial(loss_kernel, groups, shards, negatives,...  8.64 us
    unnamed x9, local copies, waits for them, and re-layouts  3.41 us

profile of v1, /device:TPU:0, one launch (start us, length us, event | category | flops | bytes accessed | tf_op | source)
XLA Modules:
  0.0 83.2 jit_solution(14932715673843980145)
XLA Ops:
  0.6 0.7 add_convert_fusion
  1.4 0.1 pad.8.clone
  1.5 0.7 convert_reduce_fusion.1
  2.2 0.7 convert_reduce_fusion
  2.9 0.7 maximum_maximum_fusion.meta_ref
  3.6 1.0 %slice.9 = bf16[32,1,768]{2,1,0:T(2,128)(2,1)S(1)} slice(bf16[32,64,768]{2,1,0:T(8,128)(2,1)} %store_ref.1), slice={[0:32], [0:1], [0:768]} | slice | bytes 98304 | tf_op jit(solution)/shard_map/slice | solution.py:486
  4.6 0.6 copy.14
  5.3 0.0 copy-start
  5.3 66.5 %exchange.1 = (f32[4,32,128]{2,1,0:T(8,128)}, bf16[8,32,768]{2,1,0:T(8,128)(2,1)}, f32[32,1,8,256]{3,2,1,0:T(8,128)}) custom-call(bf16[1,32,768]{2,1,0:T(8,128)(2,1)} %query_ref.1, bf16[1,64,768]{2,1,0:T(8,128)(2,1)} %positive_ref.1, bf16[32,768]{1,0:T(8,128)(2,1)} %bitcast.8, f32[1,8,256]{2,1,0:T(8,128)} %maximum_maximum_fusion.meta_ref, ...), custom_call_target="tpu_custom_call" | custom-call | tf_op jit(solution)/shard_map/exchange/pallas_call | solution.py:491
  71.8 0.0 copy-done
  71.8 0.0 copy-start.1
  71.8 1.0 %copy-done.1 = bf16[8,32,768]{2,1,0:T(8,128)(2,1)S(1)} copy-done((bf16[8,32,768]{2,1,0:T(8,128)(2,1)S(1)}, bf16[8,32,768]{2,1,0:T(8,128)(2,1)}, u32[]{:S(2)}) %copy-start.1) | copy-done | bytes 393240
  72.8 0.0 copy-start.2
  72.8 0.9 %copy-done.2 = f32[32,1,8,256]{3,2,1,0:T(8,128)S(1)} copy-done((f32[32,1,8,256]{3,2,1,0:T(8,128)S(1)}, f32[32,1,8,256]{3,2,1,0:T(8,128)}, u32[]{:S(2)}) %copy-start.2) | copy-done | bytes 262168
  73.7 0.0 copy-start.3
  73.7 0.8 %copy-done.3 = f32[4,32,128]{2,1,0:T(8,128)S(1)} copy-done((f32[4,32,128]{2,1,0:T(8,128)S(1)}, f32[4,32,128]{2,1,0:T(8,128)}, u32[]{:S(2)}) %copy-start.3) | copy-done | bytes 65560
  74.6 8.6 %loss.1 = (f32[1,8]{1,0:T(1,128)}, f32[768,768]{1,0:T(8,128)}) custom-call(f32[4,32,128]{2,1,0:T(8,128)S(1)} %copy-done.3, bf16[8,32,768]{2,1,0:T(8,128)(2,1)S(1)} %copy-done.1, f32[32,8,256]{2,1,0:T(8,128)S(1)} %bitcast.7, bf16[768,768]{1,0:T(8,128)(2,1)S(1)} %copy-done), custom_call_target="tpu_custom_call" | custom-call | tf_op jit(solution)/shard_map/loss/pallas_call | solution.py:536
  (3 shorter events, 0.0 us)
Async XLA Ops:
  5.3 66.5 %copy-start = (bf16[768,768]{1,0:T(8,128)(2,1)S(1)}, bf16[768,768]{1,0:T(8,128)(2,1)}, u32[]{:S(2)}) copy-start(bf16[768,768]{1,0:T(8,128)(2,1)} %dense_ref.1) | copy-start | bytes 3538948
  71.8 1.0 %copy-start.1 = (bf16[8,32,768]{2,1,0:T(8,128)(2,1)S(1)}, bf16[8,32,768]{2,1,0:T(8,128)(2,1)}, u32[]{:S(2)}) copy-start(bf16[8,32,768]{2,1,0:T(8,128)(2,1)} %get-tuple-element.6.cls_ref) | copy-start | bytes 1179652
  72.8 0.9 %copy-start.2 = (f32[32,1,8,256]{3,2,1,0:T(8,128)S(1)}, f32[32,1,8,256]{3,2,1,0:T(8,128)}, u32[]{:S(2)}) copy-start(f32[32,1,8,256]{3,2,1,0:T(8,128)} %get-tuple-element.7) | copy-start | bytes 786436
  73.7 0.8 %copy-start.3 = (f32[4,32,128]{2,1,0:T(8,128)S(1)}, f32[4,32,128]{2,1,0:T(8,128)}, u32[]{:S(2)}) copy-start(f32[4,32,128]{2,1,0:T(8,128)} %get-tuple-element.5.tables_ref) | copy-start | bytes 196612

commit v2 on v1

--- a/solution.py
+++ b/solution.py
@@ -31,14 +31,15 @@
     lq,
     query_ref,
     positive_ref,
-    cls_ref,
-    meta_ref,
+    ids_ref,
+    teacher_ref,
     transform_ref,
     store_ref,
     vocab_ref,
     tables_out,
     cls_out,
     meta_out,
+    heads,
     hidden,
     vocab,
     cls_buf,
@@ -88,6 +89,10 @@
         store_ref.at[pl.ds(group * share, share)], hidden, load_sem.at[0]
     )
     load_vocab = pltpu.make_async_copy(vocab_ref, vocab, load_sem.at[1])
+    load_heads = pltpu.make_async_copy(
+        store_ref.at[:, pl.ds(0, heads.shape[1])], heads, load_sem.at[2]
+    )
+    load_heads.start()
     load_store.start()
     load_vocab.start()
 
@@ -102,60 +107,71 @@
 
     lax.fori_loop(1, devices, greet, 0)
 
-    def block(chunk, slot):
+    def block(chunk, half, slot):
         if chunk == 0:
-            return cls_buf.at[slot]
-        if chunk == 1:
-            return front.at[slot]
-        return coded.at[chunk - 2, slot]
-
-    def order(chunk):
+            ref = front.at[slot]
+        elif chunk == 1:
+            ref = cls_buf.at[slot]
+        else:
+            ref = coded.at[chunk - 2, slot]
+        rows = ref.shape[0] // 2
+        return ref.at[pl.ds(half * rows, rows)]
+
+    def order(half):
         outer = list(range(1, bits))
-        return (outer if chunk % 2 == 0 else outer[::-1]) + [0]
-
-    def hop(chunk, offset, dim):
-        source = cls_ref if chunk == 0 and offset == 0 else block(chunk, peers[offset])
+        return (outer if half == 0 else outer[::-1]) + [0]
+
+    def hop(chunk, half, offset, dim):
+        piece = block(chunk, half, peers[offset])
         return pltpu.make_async_remote_copy(
-            src_ref=source,
-            dst_ref=block(chunk, peers[offset]),
-            send_sem=tree_send.at[chunk, offset, dim],
-            recv_sem=tree_recv.at[chunk, offset ^ (1 << dim)],
+            src_ref=piece,
+            dst_ref=piece,
+            send_sem=tree_send.at[2 * chunk + half, offset, dim],
+            recv_sem=tree_recv.at[2 * chunk + half, offset ^ (1 << dim)],
             device_id={"shard": peers[1 << dim]},
             device_id_type=MESH_ID,
         )
 
-    def arrived(chunk, offset):
+    def arrived(chunk, half, offset):
+        piece = block(chunk, half, peers[offset])
         pltpu.make_async_remote_copy(
-            src_ref=block(chunk, peers[offset]),
-            dst_ref=block(chunk, peers[offset]),
-            send_sem=tree_send.at[chunk, 0, 0],
-            recv_sem=tree_recv.at[chunk, offset],
+            src_ref=piece,
+            dst_ref=piece,
+            send_sem=tree_send.at[2 * chunk + half, 0, 0],
+            recv_sem=tree_recv.at[2 * chunk + half, offset],
             device_id={"shard": peers[1]},
             device_id_type=MESH_ID,
         ).wait_recv()
 
     hops = []
 
-    def forward(chunk, offset):
-        path = order(chunk)
+    def forward(chunk, half, offset):
+        path = order(half)
         last = max([path.index(i) for i in range(bits) if (offset >> i) & 1], default=-1)
         for dim in path[last + 1 :]:
-            copy = hop(chunk, offset, dim)
+            copy = hop(chunk, half, offset, dim)
             copy.start()
             hops.append(copy)
 
     def relay(chunk, level):
         for offset in range(0, shards, 2):
             if offset.bit_count() == level:
-                arrived(chunk, offset)
-                forward(chunk, offset)
+                for half in range(2):
+                    arrived(chunk, half, offset)
+                    forward(chunk, half, offset)
 
     def finish(chunk):
         for offset in range(1, shards, 2):
-            arrived(chunk, offset)
+            for half in range(2):
+                arrived(chunk, half, offset)
+
+    def first_token(values):
+        values = values.astype(jnp.float32)
+        token = lax.broadcasted_iota(jnp.int32, values.shape, 1)
+        return jnp.sum(jnp.where(token == 0, values, 0.0), axis=1)
 
     def encode_chunk(chunk):
-        if chunk == 1:
+        if chunk == 0:
             rows = jnp.concatenate(
                 [
                     query_ref[...].reshape(front_query, width),
@@ -164,6 +180,20 @@
                 axis=0,
             )
             front[shard] = encode(rows, transform_ref[...])
+        elif chunk == 1:
+            load_heads.wait()
+            cls_buf[shard] = first_token(heads[...]).astype(jnp.bfloat16)
+            meta_buf[linear] = jnp.zeros(meta_buf.shape[1:], jnp.float32)
+            parts = width // LANES
+            for i, ref in enumerate((query_ref, positive_ref)):
+                states = first_token(ref[:, :8])
+                for j in range(parts):
+                    meta_buf[linear, :, i * parts + j, :] = states[:, j * LANES : (j + 1) * LANES]
+            negatives = ids_ref.shape[1]
+            meta_buf[linear, :, 2 * parts, :negatives] = ids_ref[...].astype(jnp.float32)
+            meta_buf[linear, :, 2 * parts, negatives : 2 * negatives] = teacher_ref[
+                ...
+            ].astype(jnp.float32)
         else:
             first = (chunk - 2) * chunk_passages
             rows = hidden[first : first + chunk_passages].reshape(chunk_rows, width)
@@ -229,7 +259,7 @@
     def meta_copy(i, sender):
         other = (linear + i) % devices
         return pltpu.make_async_remote_copy(
-            src_ref=meta_ref,
+            src_ref=meta_buf.at[sender],
             dst_ref=meta_buf.at[sender],
             send_sem=meta_send.at[i],
             recv_sem=meta_recv.at[i],
@@ -237,9 +267,8 @@
             device_id_type=MESH_ID,
         )
 
+    encode_chunk(0)
     encode_chunk(1)
-    cls_buf[shard] = cls_ref[...]
-    meta_buf[linear] = meta_ref[...]
     passage_pool[store_total + shards * queries :, :] = jnp.zeros(
         (passage_pool.shape[0] - store_total - shards * queries, columns), jnp.float32
     )
@@ -252,7 +281,8 @@
                 load_store.wait()
             if step >= 2:
                 encode_chunk(step)
-            forward(step, 0)
+            forward(step, 0, 0)
+            forward(step, 1, 0)
             if step == 1:
 
                 def send_meta(i, carry):
@@ -266,7 +296,7 @@
         ready = step - bits + 1
         if 0 <= ready < total:
             finish(ready)
-            if ready == 1:
+            if ready == 0:
                 load_vocab.wait()
                 pool_front()
             elif ready > 1:
@@ -465,25 +495,11 @@
     share = store_rows // groups
     chunk_passages = min(CHUNK_PASSAGES, share)
     chunks = share // chunk_passages
-    parts = width // LANES
-    rows = 2 * parts + 1
+    rows = 2 * (width // LANES) + 1
     rows += -rows % 8
     pooled = share * shards + shards * queries
     pooled += -pooled % 128
     total = devices * queries
-
-    labels = jnp.concatenate([negative_ids, teacher_margins], axis=1).astype(jnp.float32)
-    labels = jnp.pad(labels, ((0, 0), (0, LANES - 2 * negatives)))
-    meta = jnp.concatenate(
-        [
-            query_hidden[:, 0, :].astype(jnp.float32).reshape(queries, parts, LANES),
-            positive_hidden[:, 0, :].astype(jnp.float32).reshape(queries, parts, LANES),
-            labels[:, None, :],
-            jnp.zeros((queries, rows - 2 * parts - 1, LANES), jnp.float32),
-        ],
-        axis=1,
-    )
-    store_cls = passage_store[:, 0, :]
 
     vmem = pl.BlockSpec(memory_space=pltpu.VMEM)
     hbm = pl.BlockSpec(memory_space=pl.ANY)
@@ -498,6 +514,7 @@
         in_specs=[vmem] * 5 + [hbm] * 2,
         out_specs=[vmem] * 3,
         scratch_shapes=[
+            pltpu.VMEM((store_rows, 8, width), jnp.bfloat16),
             pltpu.VMEM((share, lp, width), jnp.bfloat16),
             pltpu.VMEM((width, columns), jnp.bfloat16),
             pltpu.VMEM((shards, store_rows, width), jnp.bfloat16),
@@ -508,9 +525,9 @@
             pltpu.VMEM((pooled, columns), jnp.float32),
             pltpu.VMEM((shards, total, pooled), jnp.float32),
             pltpu.VMEM((groups, total, pooled), jnp.float32),
-            dma((2,)),
-            dma((chunks + 2, shards, bits)),
-            dma((chunks + 2, shards)),
+            dma((3,)),
+            dma((2 * (chunks + 2), shards, bits)),
+            dma((2 * (chunks + 2), shards)),
             dma((devices,)),
             dma((devices,)),
             dma((groups,)),
@@ -527,8 +544,8 @@
     )(
         query_hidden,
         positive_hidden,
-        store_cls,
-        meta,
+        negative_ids,
+        teacher_margins,
         transform_weight,
         passage_store,
         vocab_weight,

time: 83.6 us -> 79.8 us (0.955)
  other arithmetic: 2.85 us -> 0 us
  local copies, waits for them, and re-layouts: 4.56 us -> 2.78 us
  Pallas kernels: 75.1 us -> 76.1 us
    convert_element_type x3 -> x0, other arithmetic: 2.19 us -> none  [the longest x1 0.75 us: body(): jnp.concatenate([negative_ids, teacher_margins], axis=1).astype(jnp.float32)]
    slice x1 -> x0, local copies, waits for them, and re-layouts: 1.05 us -> none  [body(): store_cls = passage_store[:, 0, :]]
    pallas_call x1, Pallas kernels: 66.5 us -> 67.4 us  [body(): pl.pallas_call(functools.partial(exchange_kernel, groups, shards, lq), ou...]
    unnamed x9 -> x8, local copies, waits for them, and re-layouts: 3.41 us -> 2.78 us
where the time goes in v2:
time: 79.8 us; the launch traced here: 79.5 us
  Pallas kernels  76.1 us (95%)
  local copies, waits for them, and re-layouts  2.78 us (3%)
    pallas_call x1, Pallas kernels, body(): pl.pallas_call(functools.partial(exchange_kernel, groups, shards, lq), ou...  67.4 us
    pallas_call x1, Pallas kernels, body(): pl.pallas_call(functools.partial(loss_kernel, groups, shards, negatives,...  8.64 us
    unnamed x8, local copies, waits for them, and re-layouts  2.78 us

profile of v2, /device:TPU:0, one launch (start us, length us, event | category | flops | bytes accessed | tf_op | source)
XLA Modules:
  0.0 79.5 jit_solution(12376453215460636798)
XLA Ops:
  0.6 0.0 copy-start
  0.6 67.4 %exchange.1 = (f32[4,32,128]{2,1,0:T(8,128)}, bf16[8,32,768]{2,1,0:T(8,128)(2,1)}, f32[32,1,8,256]{3,2,1,0:T(8,128)}) custom-call(bf16[1,32,768]{2,1,0:T(8,128)(2,1)} %query_ref.1, bf16[1,64,768]{2,1,0:T(8,128)(2,1)} %positive_ref.1, s32[1,8]{1,0:T(1,128)} %ids_ref.1, s32[1,8]{1,0:T(1,128)} %teacher_ref.1, bf16[768,768]{1,0:T(8,128)(2,1)} %transform_ref.1, ...), custom_call_target="tpu_custom_call" | custom-call | tf_op jit(solution)/shard_map/exchange/pallas_call | solution.py:507
  68.1 0.0 copy-done
  68.1 0.0 copy-start.1
  68.1 1.0 %copy-done.1 = bf16[8,32,768]{2,1,0:T(8,128)(2,1)S(1)} copy-done((bf16[8,32,768]{2,1,0:T(8,128)(2,1)S(1)}, bf16[8,32,768]{2,1,0:T(8,128)(2,1)}, u32[]{:S(2)}) %copy-start.1) | copy-done | bytes 393240
  69.1 0.0 copy-start.2
  69.1 0.9 %copy-done.2 = f32[32,1,8,256]{3,2,1,0:T(8,128)S(1)} copy-done((f32[32,1,8,256]{3,2,1,0:T(8,128)S(1)}, f32[32,1,8,256]{3,2,1,0:T(8,128)}, u32[]{:S(2)}) %copy-start.2) | copy-done | bytes 262168
  70.1 0.0 copy-start.3
  70.1 0.8 %copy-done.3 = f32[4,32,128]{2,1,0:T(8,128)S(1)} copy-done((f32[4,32,128]{2,1,0:T(8,128)S(1)}, f32[4,32,128]{2,1,0:T(8,128)}, u32[]{:S(2)}) %copy-start.3) | copy-done | bytes 65560
  70.9 8.6 %loss.1 = (f32[1,8]{1,0:T(1,128)}, f32[768,768]{1,0:T(8,128)}) custom-call(f32[4,32,128]{2,1,0:T(8,128)S(1)} %copy-done.3, bf16[8,32,768]{2,1,0:T(8,128)(2,1)S(1)} %copy-done.1, f32[32,8,256]{2,1,0:T(8,128)S(1)} %bitcast.1, bf16[768,768]{1,0:T(8,128)(2,1)S(1)} %copy-done), custom_call_target="tpu_custom_call" | custom-call | tf_op jit(solution)/shard_map/loss/pallas_call | solution.py:553
Async XLA Ops:
  0.6 67.5 %copy-start = (bf16[768,768]{1,0:T(8,128)(2,1)S(1)}, bf16[768,768]{1,0:T(8,128)(2,1)}, u32[]{:S(2)}) copy-start(bf16[768,768]{1,0:T(8,128)(2,1)} %dense_ref.1) | copy-start | bytes 3538948
  68.1 1.0 %copy-start.1 = (bf16[8,32,768]{2,1,0:T(8,128)(2,1)S(1)}, bf16[8,32,768]{2,1,0:T(8,128)(2,1)}, u32[]{:S(2)}) copy-start(bf16[8,32,768]{2,1,0:T(8,128)(2,1)} %get-tuple-element.6.cls_ref) | copy-start | bytes 1179652
  69.1 0.9 %copy-start.2 = (f32[32,1,8,256]{3,2,1,0:T(8,128)S(1)}, f32[32,1,8,256]{3,2,1,0:T(8,128)}, u32[]{:S(2)}) copy-start(f32[32,1,8,256]{3,2,1,0:T(8,128)} %get-tuple-element.7) | copy-start | bytes 786436
  70.1 0.8 %copy-start.3 = (f32[4,32,128]{2,1,0:T(8,128)S(1)}, f32[4,32,128]{2,1,0:T(8,128)}, u32[]{:S(2)}) copy-start(f32[4,32,128]{2,1,0:T(8,128)} %get-tuple-element.5.tables_ref) | copy-start | bytes 196612

commit v3 on v2

--- a/solution.py
+++ b/solution.py
@@ -390,14 +390,33 @@
     negatives,
     chunk_passages,
     vocab_total,
+    tables_hbm,
+    cls_hbm,
+    meta_hbm,
+    dense_hbm,
+    margin_ref,
+    grad_ref,
+    margin_buf,
     tables_ref,
     cls_ref,
     meta_ref,
     dense_ref,
-    margin_ref,
-    grad_ref,
-    margin_buf,
+    load_sem,
 ):
+    pairs = (
+        (dense_hbm, dense_ref),
+        (cls_hbm, cls_ref),
+        (meta_hbm, meta_ref),
+        (tables_hbm, tables_ref),
+    )
+    loads = [
+        pltpu.make_async_copy(source, target, load_sem.at[i])
+        for i, (source, target) in enumerate(pairs)
+    ]
+    for load in loads:
+        load.start()
+    for load in loads:
+        load.wait()
     _, store_rows, width = cls_ref.shape
     total, _, lanes = meta_ref.shape
     passages = shards * store_rows
@@ -558,10 +577,17 @@
             jax.ShapeDtypeStruct((queries, negatives), jnp.float32),
             jax.ShapeDtypeStruct((width, width), jnp.float32),
         ],
-        in_specs=[vmem] * 4,
+        in_specs=[hbm] * 4,
         out_specs=[vmem] * 2,
-        scratch_shapes=[pltpu.VMEM((total, pooled), jnp.float32)],
-        compiler_params=pltpu.CompilerParams(vmem_limit_bytes=32 * 1024 * 1024),
+        scratch_shapes=[
+            pltpu.VMEM((total, pooled), jnp.float32),
+            pltpu.VMEM((groups, total, pooled), jnp.float32),
+            pltpu.VMEM((shards, store_rows, width), jnp.bfloat16),
+            pltpu.VMEM((total, rows, LANES), jnp.float32),
+            pltpu.VMEM((width, width), jnp.bfloat16),
+            dma((4,)),
+        ],
+        compiler_params=pltpu.CompilerParams(vmem_limit_bytes=56 * 1024 * 1024),
         name="loss",
     )(tables, cls_all, meta_all.reshape(total, rows, LANES), dense_weight)
 

time: 79.8 us -> 78.4 us (0.982)
  local copies, waits for them, and re-layouts: 2.78 us -> 0 us
  Pallas kernels: 76.1 us -> 77.5 us
    unnamed x8 -> x0, local copies, waits for them, and re-layouts: 2.78 us -> none
    pallas_call x1, Pallas kernels: 8.64 us -> 10.1 us  [body(): pl.pallas_call(functools.partial(loss_kernel, groups, shards, negatives,...]
where the time goes in v3:
time: 78.4 us; the launch traced here: 78.3 us
  Pallas kernels  77.5 us (99%)
  between operations  0.8 us (1%)
    pallas_call x1, Pallas kernels, body(): pl.pallas_call(functools.partial(exchange_kernel, groups, shards, lq), ou...  67.4 us
    pallas_call x1, Pallas kernels, body(): pl.pallas_call(functools.partial(loss_kernel, groups, shards, negatives,...  10.1 us

profile of v3, /device:TPU:0, one launch (start us, length us, event | category | flops | bytes accessed | tf_op | source)
XLA Modules:
  0.0 78.3 jit_solution(12042167466982879544)
XLA Ops:
  0.6 67.4 %exchange.1 = (f32[4,32,128]{2,1,0:T(8,128)}, bf16[8,32,768]{2,1,0:T(8,128)(2,1)}, f32[32,1,8,256]{3,2,1,0:T(8,128)}) custom-call(bf16[1,32,768]{2,1,0:T(8,128)(2,1)} %query_ref.1, bf16[1,64,768]{2,1,0:T(8,128)(2,1)} %positive_ref.1, s32[1,8]{1,0:T(1,128)} %ids_ref.1, s32[1,8]{1,0:T(1,128)} %teacher_ref.1, bf16[768,768]{1,0:T(8,128)(2,1)} %transform_ref.1, ...), custom_call_target="tpu_custom_call" | custom-call | tf_op jit(solution)/shard_map/exchange/pallas_call | solution.py:526
  68.0 10.1 %loss.1 = (f32[1,8]{1,0:T(1,128)}, f32[768,768]{1,0:T(8,128)}) custom-call(f32[4,32,128]{2,1,0:T(8,128)} %get-tuple-element.5.tables_hbm, bf16[8,32,768]{2,1,0:T(8,128)(2,1)} %get-tuple-element.6.cls_hbm, f32[32,8,256]{2,1,0:T(8,128)} %bitcast.1, bf16[768,768]{1,0:T(8,128)(2,1)} %dense_hbm.1), custom_call_target="tpu_custom_call" | custom-call | tf_op jit(solution)/shard_map/loss/pallas_call | solution.py:572
